TPU v7x, 32 devices: a whole 2x2x4 slice. The times are simulated.
32 devices in a mesh: dp: 8 (over z, y), tensor: 4 (over x, core).
Axes of the slice: x: 2, y: 2, z: 4, core: 2. Of those that a mesh axis runs over, the one named last changes fastest.
Arguments:
- tokens: bfloat16 [16384, 768], P(('dp', 'tensor')), may hold values from -6 to 6
- grad_out: bfloat16 [16384, 768], P(('dp', 'tensor')), may hold values from -6 to 6
- seg_ids: int32 [16, 1024], P('dp'), may hold values from 0 to 5, never falling along the last dimension, each value on 1 to 800 neighbouring positions
- w_qkv: bfloat16 [3, 768, 768], P(None, 'dp', 'tensor'), may hold values from -0.21875 to 0.21875
- b_qv: bfloat16 [2, 768], P(None, ('tensor', 'dp')), may hold values from -3 to 3
- w_out: bfloat16 [768, 768], P('tensor', 'dp'), may hold values from -1.75 to 1.75
- w_up: bfloat16 [768, 3072], P('dp', 'tensor'), may hold values from -0.21875 to 0.21875
- b_up: bfloat16 [3072], P(('tensor', 'dp')), may hold values from -3 to 3
- w_down: bfloat16 [3072, 768], P('tensor', 'dp'), may hold values from -0.21875 to 0.21875
- b_out: float32 [768], P(('dp', 'tensor')), may hold values from -2 to 2
- b_down: float32 [768], P(('dp', 'tensor')), may hold values from -2 to 2
- g_one: float32 [768], P(('dp', 'tensor')), may hold values from 0.5 to 1.5
- s_one: float32 [768], P(('dp', 'tensor')), may hold values from -2 to 2
- g_two: float32 [768], P(('dp', 'tensor')), may hold values from 0.5 to 1.5
- s_two: float32 [768], P(('dp', 'tensor')), may hold values from -2 to 2
Outputs:
- layer_out: bfloat16 [16384, 768], P(('dp', 'tensor'))
- input_grad: bfloat16 [16384, 768], P(('dp', 'tensor'))
- grad_qkv: float32 [3, 768, 768], P(None, 'dp', 'tensor')
- grad_bias_qv: float32 [2, 768], P(None, ('tensor', 'dp'))
- grad_out_proj: float32 [768, 768], P('tensor', 'dp')
- grad_up: float32 [768, 3072], P('dp', 'tensor')
- grad_bias_up: float32 [3072], P(('tensor', 'dp'))
- grad_down: float32 [3072, 768], P('tensor', 'dp')
- grad_bias_out: float32 [768], P(('dp', 'tensor'))
- grad_bias_down: float32 [768], P(('dp', 'tensor'))
- grad_gain_one: float32 [768], P(('dp', 'tensor'))
- grad_shift_one: float32 [768], P(('dp', 'tensor'))
- grad_gain_two: float32 [768], P(('dp', 'tensor'))
- grad_shift_two: float32 [768], P(('dp', 'tensor'))
Inputs may be any that keep to these rules, and one draw needn't show every extreme that they name: `seg_ids`: within a sequence the ids never fall; each document spans 1 to 800 tokens, and the longest one of a draw spans exactly 800.
All inputs are finite; a program needn't handle non-finite values.
Results may differ from a plain program's by a relative error of at most 0.024.
Values may be sent and summed in bfloat16 or wider, within the bound.
No kernel may reach another device: no remote copies, remote signals or barrier semaphores. Data moves between devices by JAX's collectives and lax.ppermute only.
A program may use at most 128 MiB of HBM per device.

v0:
```python
import jax
import jax.numpy as jnp
from jax import lax
from jax.sharding import PartitionSpec as P

HD = 64
EPSILON = 1e-05
ROOT_HALF = 0.7071067811865476


def norm_rows(r, gain, shift):
    mean = jnp.mean(r, axis=-1, keepdims=True)
    cent = r - mean
    var = jnp.mean(cent * cent, axis=-1, keepdims=True)
    return cent * lax.rsqrt(var + EPSILON) * gain + shift


def gelu_exact(u):
    return 0.5 * u * (1.0 + lax.erf(u * ROOT_HALF))


def masked_scores(query, keys, seg_query, seg_keys):
    raw = jnp.einsum("qhd,khd->hqk", query, keys, preferred_element_type=jnp.float32)
    same = seg_query[:, None] == seg_keys[None, :]
    return jnp.where(same[None], raw * 0.125, -1000000000.0)


def attend_forward(query, keys, values, seg_query, seg_keys):
    scores = masked_scores(query, keys, seg_query, seg_keys)
    top = jnp.max(scores, axis=-1, keepdims=True)
    expo = jnp.exp(scores - top)
    total = jnp.sum(expo, axis=-1, keepdims=True)
    probs = (expo / total).astype(jnp.bfloat16)
    context = jnp.einsum("hqk,khd->qhd", probs, values, preferred_element_type=jnp.float32)
    return (context.astype(jnp.bfloat16), top + jnp.log(total))


def attend_backward(query, keys, values, seg_query, seg_keys, lse_block, d_block):
    scores = masked_scores(query, keys, seg_query, seg_keys)
    probs = jnp.exp(scores - lse_block)
    probs_low = probs.astype(jnp.bfloat16)
    d_probs = jnp.einsum("qhd,khd->hqk", d_block, values, preferred_element_type=jnp.float32)
    inner = jnp.sum(probs * d_probs, axis=-1, keepdims=True)
    d_scores = (probs * (d_probs - inner)).astype(jnp.bfloat16)
    d_query = jnp.einsum("hqk,khd->qhd", d_scores, keys, preferred_element_type=jnp.float32) * 0.125
    d_keys = jnp.einsum("hqk,qhd->khd", d_scores, query, preferred_element_type=jnp.float32) * 0.125
    d_values = jnp.einsum("hqk,qhd->khd", probs_low, d_block, preferred_element_type=jnp.float32)
    return (d_query, d_keys, d_values)


def contract_rows(left, right):
    return lax.dot_general(
        left, right, (((0,), (0,)), ((), ())), preferred_element_type=jnp.float32
    )


def contract_cols(left, right):
    return lax.dot_general(
        left, right, (((1,), (1,)), ((), ())), preferred_element_type=jnp.float32
    )


def local(
    tokens,
    grad_out,
    seg_ids,
    w_qkv,
    b_qv,
    w_out,
    w_up,
    b_up,
    w_down,
    b_out,
    b_down,
    g_one,
    s_one,
    g_two,
    s_two,
):
    seqs, seq_len = seg_ids.shape
    group = seqs * seq_len
    block = min(512, seq_len)
    nblocks = seq_len // block
    items = seqs * nblocks
    wqkv_l, bqv_l, wout_l, wup_l, bup_l, wdown_l = (
        lax.all_gather(w_qkv, "dp", axis=1, tiled=True),
        lax.all_gather(b_qv, "dp", axis=1, tiled=True),
        lax.all_gather(w_out, "dp", axis=1, tiled=True),
        lax.all_gather(w_up, "dp", axis=0, tiled=True),
        lax.all_gather(b_up, "dp", axis=0, tiled=True),
        lax.all_gather(w_down, "dp", axis=1, tiled=True),
    )
    bout_f, bdown_f, gone_f, sone_f, gtwo_f, stwo_f = (
        lax.all_gather(b_out, ("dp", "tensor"), axis=0, tiled=True),
        lax.all_gather(b_down, ("dp", "tensor"), axis=0, tiled=True),
        lax.all_gather(g_one, ("dp", "tensor"), axis=0, tiled=True),
        lax.all_gather(s_one, ("dp", "tensor"), axis=0, tiled=True),
        lax.all_gather(g_two, ("dp", "tensor"), axis=0, tiled=True),
        lax.all_gather(s_two, ("dp", "tensor"), axis=0, tiled=True),
    )
    local_width = wqkv_l.shape[2]
    local_heads = local_width // HD
    x_full = lax.all_gather(tokens, "tensor", axis=0, tiled=True)
    proj = jnp.einsum("td,jde->jte", x_full, wqkv_l, preferred_element_type=jnp.float32)
    biases = jnp.stack([bqv_l[0], jnp.zeros_like(bqv_l[0]), bqv_l[1]]).astype(jnp.float32)
    proj = (proj + biases[:, None, :]).astype(jnp.bfloat16)
    heads = proj.reshape(3, seqs, seq_len, local_heads, HD)
    queries = heads[0].reshape(items, block, local_heads, HD)
    seg_blocks = seg_ids.reshape(items, block)
    owner = jnp.arange(items, dtype=jnp.int32) // nblocks

    def forward_item(item):
        query, seg_query, which = item
        return attend_forward(query, heads[1][which], heads[2][which], seg_query, seg_ids[which])

    context, lse = lax.map(forward_item, (queries, seg_blocks, owner))
    context = context.reshape(group, local_width)
    part = context
    attn = (
        lax.psum_scatter(
            jnp.dot(part, wout_l, preferred_element_type=jnp.float32).astype(jnp.bfloat16),
            "tensor",
            scatter_dimension=0,
            tiled=True,
        ).astype(jnp.float32)
        + bout_f
    )
    first = tokens.astype(jnp.float32) + attn
    normed = norm_rows(first, gone_f, sone_f)
    normed_full = lax.all_gather(normed.astype(jnp.bfloat16), "tensor", axis=0, tiled=True)
    up = jnp.dot(normed_full, wup_l, preferred_element_type=jnp.float32) + bup_l.astype(jnp.float32)
    hidden = gelu_exact(up).astype(jnp.bfloat16)
    part = hidden
    branch = (
        lax.psum_scatter(
            jnp.dot(part, wdown_l, preferred_element_type=jnp.float32).astype(jnp.bfloat16),
            "tensor",
            scatter_dimension=0,
            tiled=True,
        ).astype(jnp.float32)
        + bdown_f
    )
    second = normed + branch
    layer_out = norm_rows(second, gtwo_f, stwo_f)
    wqkv_b, wout_b, wup_b, wdown_b = (
        lax.all_gather(w_qkv, "dp", axis=1, tiled=True),
        lax.all_gather(w_out, "dp", axis=1, tiled=True),
        lax.all_gather(w_up, "dp", axis=0, tiled=True),
        lax.all_gather(w_down, "dp", axis=1, tiled=True),
    )
    _, pull_two = jax.vjp(norm_rows, second, gtwo_f, stwo_f)
    d_second, d_gain_two, d_shift_two = pull_two(grad_out.astype(jnp.float32))
    d_branch = d_second.astype(jnp.bfloat16)
    d_bias_down = jnp.sum(d_branch.astype(jnp.float32), axis=0)
    branch_full = lax.all_gather(d_branch, "tensor", axis=0, tiled=True)
    grad_down_w = contract_rows(hidden, branch_full)
    d_hidden = contract_cols(branch_full, wdown_b)
    _, pull_gelu = jax.vjp(gelu_exact, up)
    d_up = pull_gelu(d_hidden)[0].astype(jnp.bfloat16)
    grad_bias_up = jnp.sum(d_up.astype(jnp.float32), axis=0)
    grad_up_w = contract_rows(normed_full, d_up)
    part = d_up
    d_normed = d_second + lax.psum_scatter(
        contract_cols(part, wup_b).astype(jnp.bfloat16), "tensor", scatter_dimension=0, tiled=True
    ).astype(jnp.float32)
    _, pull_one = jax.vjp(norm_rows, first, gone_f, sone_f)
    d_first, d_gain_one, d_shift_one = pull_one(d_normed)
    d_attn = d_first.astype(jnp.bfloat16)
    d_bias_out = jnp.sum(d_attn.astype(jnp.float32), axis=0)
    attn_full = lax.all_gather(d_attn, "tensor", axis=0, tiled=True)
    grad_out_w = contract_rows(context, attn_full)
    d_context = contract_cols(attn_full, wout_b).astype(jnp.bfloat16)
    d_ctx_blocks = d_context.reshape(items, block, local_heads, HD)

    def backward_item(item):
        query, seg_query, which, lse_block, d_block = item
        return attend_backward(
            query, heads[1][which], heads[2][which], seg_query, seg_ids[which], lse_block, d_block
        )

    d_query, d_keys, d_values = lax.map(
        backward_item, (queries, seg_blocks, owner, lse, d_ctx_blocks)
    )
    d_keys = jnp.sum(d_keys.reshape(seqs, nblocks, seq_len, local_heads, HD), axis=1)
    d_values = jnp.sum(d_values.reshape(seqs, nblocks, seq_len, local_heads, HD), axis=1)
    d_proj = jnp.stack(
        [
            d_query.reshape(group, local_width),
            d_keys.reshape(group, local_width),
            d_values.reshape(group, local_width),
        ]
    ).astype(jnp.bfloat16)
    proj_sums = jnp.sum(d_proj.astype(jnp.float32), axis=1)
    grad_bias_qv = jnp.stack([proj_sums[0], proj_sums[2]])
    grad_qkv_w = jnp.einsum("td,jte->jde", x_full, d_proj, preferred_element_type=jnp.float32)
    part = d_proj
    d_tokens = d_first + lax.psum_scatter(
        jnp.einsum("jte,jde->td", part, wqkv_b, preferred_element_type=jnp.float32).astype(
            jnp.bfloat16
        ),
        "tensor",
        scatter_dimension=0,
        tiled=True,
    ).astype(jnp.float32)
    g_qkv, g_bqv, g_out, g_up, g_bup, g_down = (
        lax.psum_scatter(grad_qkv_w, "dp", scatter_dimension=1, tiled=True),
        lax.psum_scatter(grad_bias_qv, "dp", scatter_dimension=1, tiled=True),
        lax.psum_scatter(grad_out_w, "dp", scatter_dimension=1, tiled=True),
        lax.psum_scatter(grad_up_w, "dp", scatter_dimension=0, tiled=True),
        lax.psum_scatter(grad_bias_up, "dp", scatter_dimension=0, tiled=True),
        lax.psum_scatter(grad_down_w, "dp", scatter_dimension=1, tiled=True),
    )
    g_bout, g_bdown, g_gone, g_sone, g_gtwo, g_stwo = (
        lax.psum_scatter(d_bias_out, ("dp", "tensor"), scatter_dimension=0, tiled=True),
        lax.psum_scatter(d_bias_down, ("dp", "tensor"), scatter_dimension=0, tiled=True),
        lax.psum_scatter(d_gain_one, ("dp", "tensor"), scatter_dimension=0, tiled=True),
        lax.psum_scatter(d_shift_one, ("dp", "tensor"), scatter_dimension=0, tiled=True),
        lax.psum_scatter(d_gain_two, ("dp", "tensor"), scatter_dimension=0, tiled=True),
        lax.psum_scatter(d_shift_two, ("dp", "tensor"), scatter_dimension=0, tiled=True),
    )
    return (
        layer_out.astype(jnp.bfloat16),
        d_tokens.astype(jnp.bfloat16),
        g_qkv,
        g_bqv,
        g_out,
        g_up,
        g_bup,
        g_down,
        g_bout,
        g_bdown,
        g_gone,
        g_sone,
        g_gtwo,
        g_stwo,
    )


def solution(mesh):
    return jax.shard_map(
        local,
        mesh=mesh,
        in_specs=(
            P(("dp", "tensor"), None),
            P(("dp", "tensor"), None),
            P("dp", None),
            P(None, "dp", "tensor"),
            P(None, ("tensor", "dp")),
            P("tensor", "dp"),
            P("dp", "tensor"),
            P(("tensor", "dp")),
            P("tensor", "dp"),
            P(("dp", "tensor")),
            P(("dp", "tensor")),
            P(("dp", "tensor")),
            P(("dp", "tensor")),
            P(("dp", "tensor")),
            P(("dp", "tensor")),
        ),
        out_specs=(
            P(("dp", "tensor"), None),
            P(("dp", "tensor"), None),
            P(None, "dp", "tensor"),
            P(None, ("tensor", "dp")),
            P("tensor", "dp"),
            P("dp", "tensor"),
            P(("tensor", "dp")),
            P("tensor", "dp"),
            P(("dp", "tensor")),
            P(("dp", "tensor")),
            P(("dp", "tensor")),
            P(("dp", "tensor")),
            P(("dp", "tensor")),
            P(("dp", "tensor")),
        ),
        check_vma=False,
    )
```

profile of v0, /device:TPU:0, one launch (start us, length us, event | category | flops | bytes accessed | tf_op | source)
XLA Modules:
  0.0 854.5 jit_solution(17377182914923498748)
XLA Ops:
  8.8 22.3 %all-gather = bf16[8,24,2]{1,2,0:T(2,128)(2,1)S(1)} all-gather(bf16[1,24,2]{1,2,0:T(2,128)(2,1)} %bitcast.205), channel_id=1, replica_groups=mesh['dp'=8,'tensor'=4] {'dp'}, dimensions={0}, use_global_device_ids=true | all-gather | bytes 864 | tf_op jit(solution)/shard_map/all_gather | solution.py:87
  34.5 31.1 %all_gather.55 = bf16[192,768]{0,1:T(8,128)(2,1)S(1)} all-gather(bf16[192,96]{0,1:T(8,128)(2,1)S(1)} %copy.55), channel_id=1, replica_groups=mesh['dp'=8,'tensor'=4] {'dp'}, dimensions={1}, use_global_device_ids=true | all-gather | bytes 331776 | tf_op jit(solution)/shard_map/all_gather | solution.py:88
  65.6 35.3 %all_gather.52 = bf16[3,768,192]{2,0,1:T(4,128)(2,1)} all-gather(bf16[3,96,192]{2,0,1:T(4,128)(2,1)S(1)} %copy.49), channel_id=1, replica_groups=mesh['dp'=8,'tensor'=4] {'dp'}, dimensions={1}, use_global_device_ids=true | all-gather | bytes 995328 | tf_op jit(solution)/shard_map/all_gather | solution.py:86
  114.2 40.8 %while.26 = (s32[]{:T(128)}, bf16[4,512,3,64]{1,3,2,0:T(8,128)(2,1)}, f32[4,3,512,1]{2,1,3,0:T(4,128)}, bf16[3,2,1024,3,64]{2,4,3,1,0:T(8,128)(2,1)S(1)}, s32[4]...) while((s32[]{:T(128)}, ...), condition=%wide.region_3.4_spmd, body=%wide.region_0.3_spmd.sunk | while | flops 422148608 | bytes 25370816 | solution.py:116
  168.5 39.5 %all-reduce.16 = (f32[768]{0:T(1024)}, f32[768]{0:T(1024)}, f32[768]{0:T(1024)S(1)}, f32[768]{0:T(1024)}, f32[768]{0:T(1024)}) all-reduce(f32[768]{0:T(1024)} %dynamic-update-slice.2, f32[768]{0:T(1024)} %dynamic-update-slice.1, f32[768]{0:T(1024)} %dynamic-update-slice, ...), channel_id=1, replica_groups=mesh['dp'=8,'tensor'=4] {'dp','tensor'}, use_global_device_ids=true, to_apply=%add.2 | all-reduce | flops 3840 | bytes 30720
  218.3 21.6 %all-reduce.3 = bf16[768]{0:T(1024)(128)(2,1)} all-reduce(bf16[768]{0:T(1024)(128)(2,1)} %dynamic-update-slice.3), channel_id=1, replica_groups=mesh['dp'=8,'tensor'=4] {'dp'}, use_global_device_ids=true, to_apply=%add.3 | all-reduce | flops 768 | bytes 3072
  243.2 7.0 multiply_convert_fusion.1
  250.1 36.9 %all-gather.14.cloned.1.call-done = bf16[768,768]{0,1:T(8,128)(2,1)} async-done(((bf16[768,96]{0,1:T(8,128)(2,1)}), bf16[768,768]{0,1:T(8,128)(2,1)}) %all-gather.14.cloned.1.call-update) | async-done | bytes 1179664 | tf_op jit(solution)/shard_map/all_gather | solution.py:91
  287.0 6.5 convolution_convert_fusion.1
  293.6 36.3 %reduce-scatter.16.cloned.1.call-done = bf16[512,768]{1,0:T(8,128)(2,1)} async-done(((bf16[2048,768]{1,0:T(8,128)(2,1)}), bf16[512,768]{1,0:T(8,128)(2,1)}) %reduce-scatter.16.cloned.1.call-update) | async-done | bytes 786448 | tf_op jit(solution)/shard_map/reduce_scatter | solution.py:135
  337.4 28.6 %all-gather.16.cloned.1.call-done = bf16[2048,768]{1,0:T(8,128)(2,1)} async-done(((bf16[512,768]{1,0:T(8,128)(2,1)}), bf16[2048,768]{1,0:T(8,128)(2,1)}) %all-gather.16.cloned.1.call-update) | async-done | bytes 3145744 | tf_op jit(solution)/shard_map/all_gather | solution.py:155
  366.0 8.0 convert_reduce_fusion
  379.8 37.9 %reduce-scatter.18.cloned.1.call-done = bf16[512,768]{1,0:T(8,128)(2,1)} async-done(((bf16[2048,768]{1,0:T(8,128)(2,1)}), bf16[512,768]{1,0:T(8,128)(2,1)}) %reduce-scatter.18.cloned.1.call-update) | async-done | bytes 786448 | tf_op jit(solution)/shard_map/reduce_scatter | solution.py:163
  426.3 28.4 %all-gather.18.cloned.1.call-done = bf16[2048,768]{1,0:T(8,128)(2,1)} async-done(((bf16[512,768]{1,0:T(8,128)(2,1)}), bf16[2048,768]{1,0:T(8,128)(2,1)}) %all-gather.18.cloned.1.call-update) | async-done | bytes 3145744 | tf_op jit(solution)/shard_map/all_gather | solution.py:170
  463.9 61.6 %while.27 = (s32[]{:T(128)}, bf16[4,512,3,64]{1,3,2,0:T(8,128)(2,1)}, f32[4,1024,3,64]{1,3,2,0:T(8,128)}, f32[4,1024,3,64]{1,3,2,0:T(8,128)}, bf16[3,2,1024,3,64...) while((s32[]{:T(128)}, ...), condition=%wide.region_17.18_spmd, body=%wide.region_15.17_spmd.sunk | while | flops 1031043584 | bytes 65866036 | solution.py:181
  547.7 6.0 fusion.67
  568.6 7.0 fusion.86
  575.7 6.9 fusion.87
  584.4 40.5 %all-reduce.15 = (f32[768]{0:T(1024)S(1)}, f32[768]{0:T(1024)S(1)}, f32[768]{0:T(1024)S(1)}, f32[768]{0:T(1024)S(1)}, f32[768]{0:T(1024)S(1)}, /*index=5*/f32[768]{0:T(1024)S(1)}, f32[768]{0:T(1024)S(1)}) all-reduce(f32[768]{0:T(1024)S(1)} %dynamic-update-slice.6, ...), channel_id=1, replica_groups=mesh['dp'=8,'tensor'=4] {'dp','tensor'}, use_global_device_ids=true, to_apply=%add.6 | all-reduce | flops 5376 | bytes 43008
  630.0 21.5 %all-reduce.17 = (f32[2,192]{1,0:T(2,128)S(1)}, f32[768]{0:T(1024)S(1)}) all-reduce(f32[2,192]{1,0:T(2,128)S(1)} %pad_maximum_fusion, f32[768]{0:T(1024)S(1)} %copy-done.40), channel_id=7, replica_groups=mesh['dp'=8,'tensor'=4] {'dp'}, use_global_device_ids=true, to_apply=%region_23.24.clone | all-reduce | flops 1152 | bytes 9216
  654.3 8.0 reduce-scatter.26.cloned.1.call-done
  664.2 37.5 %reduce-scatter.20.cloned.1.call-done = bf16[512,768]{1,0:T(8,128)(2,1)} async-done(((bf16[2048,768]{1,0:T(8,128)(2,1)}), bf16[512,768]{1,0:T(8,128)(2,1)}) %reduce-scatter.20.cloned.1.call-update) | async-done | bytes 786448 | tf_op jit(solution)/shard_map/reduce_scatter | solution.py:197
  704.0 70.6 %reduce-scatter.22.cloned.1.call-done = f32[96,768]{1,0:T(8,128)} async-done(((f32[768,768]{1,0:T(8,128)}), f32[96,768]{1,0:T(8,128)}) %reduce-scatter.22.cloned.1.call-update) | async-done | bytes 294928 | tf_op jit(solution)/shard_map/reduce_scatter | solution.py:209
  774.6 72.4 %reduce-scatter.24.cloned.1.call-done = f32[768,96]{0,1:T(8,128)} async-done(((f32[768,768]{0,1:T(8,128)}), f32[768,96]{0,1:T(8,128)}) %reduce-scatter.24.cloned.1.call-update) | async-done | bytes 294928 | tf_op jit(solution)/shard_map/reduce_scatter | solution.py:211
  (319 shorter events, 210.4 us)
Async XLA Ops:
  8.0 92.9 %all-gather.8.cloned.1.call-start = ((), (), s32[]{:S(2)}) async-start(), calls=%async_computation.8 | async-start | bytes 3932160 | tf_op jit(solution)/shard_map/all_gather | solution.py:103
  8.7 199.3 %reduce-scatter.14.cloned.1.call-start = ((), (), s32[]{:S(2)}) async-start(), calls=%async_computation.9 | async-start | bytes 3932160 | tf_op jit(solution)/shard_map/reduce_scatter | solution.py:120
  155.1 5.8 copy-start.21
  160.9 47.1 %copy-start.2 = (bf16[512,768]{1,0:T(8,128)(2,1)S(1)}, bf16[512,768]{1,0:T(8,128)(2,1)}, u32[]{:S(2)}) copy-start(bf16[512,768]{1,0:T(8,128)(2,1)} %param.19) | copy-start | bytes 2359300
  160.9 80.3 %all-gather.12.cloned.1.call-start = ((), (), s32[]{:S(2)}) async-start(), calls=%async_computation.11 | async-start | bytes 1327104 | tf_op jit(solution)/shard_map/all_gather | solution.py:89
  161.5 81.7 %all-gather.10.cloned.1.call-start = ((), (), s32[]{:S(2)}) async-start(), calls=%async_computation.10 | async-start | bytes 3932160 | tf_op jit(solution)/shard_map/all_gather | solution.py:130
  213.7 73.3 %all-gather.14.cloned.1.call-start = ((), (), s32[]{:S(2)}) async-start(), calls=%async_computation.12 | async-start | bytes 1327104 | tf_op jit(solution)/shard_map/all_gather | solution.py:91
  214.3 115.7 %reduce-scatter.16.cloned.1.call-start = ((), (), s32[]{:S(2)}) async-start(), calls=%async_computation.13 | async-start | bytes 3932160 | tf_op jit(solution)/shard_map/reduce_scatter | solution.py:135
  293.5 72.5 %all-gather.16.cloned.1.call-start = ((), (), s32[]{:S(2)}) async-start(), calls=%async_computation.14 | async-start | bytes 3932160 | tf_op jit(solution)/shard_map/all_gather | solution.py:155
  337.3 80.4 %reduce-scatter.18.cloned.1.call-start = ((), (), s32[]{:S(2)}) async-start(), calls=%async_computation.15 | async-start | bytes 3932160 | tf_op jit(solution)/shard_map/reduce_scatter | solution.py:163
  366.0 9.7 %copy-start.41 = (bf16[768,768]{1,0:T(8,128)(2,1)S(1)}, bf16[768,768]{1,0:T(8,128)(2,1)}, u32[]{:S(2)}) copy-start(bf16[768,768]{1,0:T(8,128)(2,1)} %all-gather.12.cloned.1.call-done) | copy-start | bytes 3538948
  379.7 75.0 %all-gather.18.cloned.1.call-start = ((), (), s32[]{:S(2)}) async-start(), calls=%async_computation.16 | async-start | bytes 3932160 | tf_op jit(solution)/shard_map/all_gather | solution.py:170
  426.1 226.6 %reduce-scatter.28.cloned.1.call-start = ((), (), s32[]{:S(2)}) async-start(), calls=%async_computation.21 | async-start | bytes 884736
  458.7 5.2 copy-start.44
  530.0 132.3 %reduce-scatter.26.cloned.1.call-start = ((), (), s32[]{:S(2)}) async-start(), calls=%async_computation.20 | async-start | bytes 2211840
  547.7 15.0 %copy-start.11 = (bf16[3,2048,192]{1,2,0:T(8,128)(2,1)}, bf16[3,2048,192]{1,2,0:T(8,128)(2,1)S(1)}, u32[]{:S(2)}) copy-start(bf16[3,2048,192]{1,2,0:T(8,128)(2,1)S(1)} %constant_dynamic-update-slice_fusion) | copy-start | bytes 7077892
  562.7 139.1 %reduce-scatter.20.cloned.1.call-start = ((), (), s32[]{:S(2)}) async-start(), calls=%async_computation.17 | async-start | bytes 3932160 | tf_op jit(solution)/shard_map/reduce_scatter | solution.py:197
  568.3 206.3 %reduce-scatter.22.cloned.1.call-start = ((), (), s32[]{:S(2)}) async-start(), calls=%async_computation.18 | async-start | bytes 2654208 | tf_op jit(solution)/shard_map/reduce_scatter | solution.py:209
  575.6 271.4 %reduce-scatter.24.cloned.1.call-start = ((), (), s32[]{:S(2)}) async-start(), calls=%async_computation.19 | async-start | bytes 2654208 | tf_op jit(solution)/shard_map/reduce_scatter | solution.py:211
  582.6 45.8 %copy-start.1 = (f32[512,768]{1,0:T(8,128)S(1)}, f32[512,768]{1,0:T(8,128)}, u32[]{:S(2)}) copy-start(f32[512,768]{1,0:T(8,128)} %copy-done) | copy-start | bytes 4718596
  582.6 45.7 %copy-start.26 = (f32[512]{0:T(512)S(1)}, f32[512]{0:T(512)}, u32[]{:S(2)}) copy-start(f32[512]{0:T(512)} %copy-done.25) | copy-start | bytes 6148
  582.6 45.7 %copy-start.28 = (f32[768]{0:T(1024)S(1)}, f32[768]{0:T(1024)}, u32[]{:S(2)}) copy-start(f32[768]{0:T(1024)} %get-tuple-element.275) | copy-start | bytes 9220
  582.7 45.7 %copy-start.31 = (f32[512]{0:T(512)S(1)}, f32[512]{0:T(512)}, u32[]{:S(2)}) copy-start(f32[512]{0:T(512)} %copy-done.30) | copy-start | bytes 6148
  629.6 72.1 %copy-start.10 = (f32[512,768]{1,0:T(8,128)S(1)}, f32[512,768]{1,0:T(8,128)}, u32[]{:S(2)}) copy-start(f32[512,768]{1,0:T(8,128)} %copy-done.9) | copy-start | bytes 4718596
  (45 other events, 105.9 us)
Sparse Core Ops, SparseCore 0:
  10.4 31.2 all-gather.7
  161.0 36.9 reduce-scatter.13
  337.5 28.5 all-gather.15
  426.2 28.5 all-gather.17
Sparse Core Ops, SparseCore 1:
  163.6 40.2 all-gather.11
  213.8 29.3 all-gather.9
  245.4 41.5 all-gather.13
  293.6 36.3 reduce-scatter.15
  379.8 37.8 reduce-scatter.17
  530.1 62.5 reduce-scatter.27
  596.0 66.3 reduce-scatter.25
  664.9 36.8 reduce-scatter.19
  705.7 68.9 reduce-scatter.21
  778.7 68.2 reduce-scatter.23
where the time goes:
time: 865 us; the launch traced here: 855 us
  waiting for transfers between devices  361 us (42%)
  blocking collectives  212 us (25%)
  matrix products  120 us (14%)
  local copies, waits for them, and re-layouts  79.5 us (9%)
  other arithmetic  47.5 us (5%)
  between operations  18.4 us (2%)
  loops' own time  16 us (2%)
    unnamed x4, blocking collectives  123 us
    reduce_scatter x1, waiting for transfers between devices, local(): lax.psum_scatter(grad_down_w, 'dp', scatter_dimension=1, tiled=True)  72.4 us
    reduce_scatter x1, waiting for transfers between devices, local(): lax.psum_scatter(grad_up_w, 'dp', scatter_dimension=0, tiled=True)  70.6 us
    reduce_scatter x1, waiting for transfers between devices, local(): lax.psum_scatter(contract_cols(part, wup_b).astype(jnp.bfloat16), 'tensor...  37.9 us
    reduce_scatter x1, waiting for transfers between devices, local(): lax.psum_scatter(jnp.einsum('jte,jde->td', part, wqkv_b, preferred_elemen...  37.5 us
    unnamed x120, local copies, waits for them, and re-layouts  37.3 us
    all_gather x1, waiting for transfers between devices, local(): lax.all_gather(w_down, 'dp', axis=1, tiled=True)  36.9 us
    reduce_scatter x1, waiting for transfers between devices, local(): lax.psum_scatter(jnp.dot(part, wdown_l, preferred_element_type=jnp.float3...  36.3 us
  transfers between devices with their start and end apart: 14, of which 10 were waited for; matrix products, arithmetic and copies ran while one was open for 11% of the time, Pallas kernels for 0%

commit v1 on v0

--- a/solution.py
+++ b/solution.py
@@ -152,7 +152,20 @@
     d_second, d_gain_two, d_shift_two = pull_two(grad_out.astype(jnp.float32))
     d_branch = d_second.astype(jnp.bfloat16)
     d_bias_down = jnp.sum(d_branch.astype(jnp.float32), axis=0)
-    branch_full = lax.all_gather(d_branch, "tensor", axis=0, tiled=True)
+
+    def render_the_panel(x_local, along_axis):
+        n_shards = lax.axis_size(along_axis)
+        local_now = sorted(((dev_i, (dev_i + 1) % n_shards) for dev_i in range(n_shards)))
+        heard = x_local
+        by_rank = [heard]
+        for dev in range(1, n_shards):
+            heard = lax.ppermute(heard, along_axis, perm=local_now)
+            by_rank.insert(0, heard)
+        near = jnp.concatenate(by_rank, axis=0)
+        current_arr = lax.axis_index(along_axis) + 1
+        return jnp.roll(near, current_arr * x_local.shape[0], axis=0)
+
+    branch_full = render_the_panel(d_branch, "tensor")
     grad_down_w = contract_rows(hidden, branch_full)
     d_hidden = contract_cols(branch_full, wdown_b)
     _, pull_gelu = jax.vjp(gelu_exact, up)

time: 865 us -> 880 us (1.017)
  local copies, waits for them, and re-layouts: 79.5 us -> 88.9 us
  starting transfers between devices: 1.23 us -> 10.6 us
    ppermute x0 -> x3, waiting for transfers between devices: none -> 34.6 us  [render_the_panel(): heard = lax.ppermute(heard, along_axis, perm=local_now)]
    all_gather x1 -> x0, waiting for transfers between devices: 28.6 us -> none  [local(): branch_full = lax.all_gather(d_branch, 'tensor', axis=0, tiled=True)]
    all_gather x1, starting transfers between devices: 0.04 us -> 9.57 us  [local(): attn_full = lax.all_gather(d_attn, 'tensor', axis=0, tiled=True)]
    reduce_scatter x1, waiting for transfers between devices: 37.9 us -> 28.5 us  [local(): lax.psum_scatter(contract_cols(part, wup_b).astype(jnp.bfloat16), 'tensor...]
    unnamed x120 -> x139, local copies, waits for them, and re-layouts: 37.3 us -> 44.1 us
  transfers between devices with their start and end apart: 14 -> 16, of which waited for: 10 -> 12; matrix products, arithmetic and copies ran while one was open for 11% -> 10% of each run, Pallas kernels for 0% -> 0%
where the time goes in v1:
time: 880 us; the launch traced here: 869 us
  waiting for transfers between devices  357 us (41%)
  blocking collectives  211 us (24%)
  matrix products  121 us (14%)
  local copies, waits for them, and re-layouts  88.9 us (10%)
  other arithmetic  46.5 us (5%)
  between operations  18.5 us (2%)
  loops' own time  16 us (2%)
  starting transfers between devices  10.6 us (1%)
    unnamed x4, blocking collectives  123 us
    reduce_scatter x1, waiting for transfers between devices, local(): lax.psum_scatter(grad_down_w, 'dp', scatter_dimension=1, tiled=True)  72.3 us
    reduce_scatter x1, waiting for transfers between devices, local(): lax.psum_scatter(grad_up_w, 'dp', scatter_dimension=0, tiled=True)  70.6 us
    unnamed x139, local copies, waits for them, and re-layouts  44.1 us
    reduce_scatter x1, waiting for transfers between devices, local(): lax.psum_scatter(jnp.einsum('jte,jde->td', part, wqkv_b, preferred_elemen...  37.5 us
    all_gather x1, waiting for transfers between devices, local(): lax.all_gather(w_down, 'dp', axis=1, tiled=True)  36.9 us
    reduce_scatter x1, waiting for transfers between devices, local(): lax.psum_scatter(jnp.dot(part, wdown_l, preferred_element_type=jnp.float3...  36.3 us
    all_gather x1, blocking collectives, local(): lax.all_gather(w_qkv, 'dp', axis=1, tiled=True)  35.3 us
  transfers between devices with their start and end apart: 16, of which 12 were waited for; matrix products, arithmetic and copies ran while one was open for 10% of the time, Pallas kernels for 0%

profile of v1, /device:TPU:0, one launch (start us, length us, event | category | flops | bytes accessed | tf_op | source)
XLA Modules:
  0.0 869.4 jit_solution(6023441578728153)
XLA Ops:
  8.8 22.3 %all-gather = bf16[8,24,2]{1,2,0:T(2,128)(2,1)S(1)} all-gather(bf16[1,24,2]{1,2,0:T(2,128)(2,1)} %bitcast.203), channel_id=1, replica_groups=mesh['dp'=8,'tensor'=4] {'dp'}, dimensions={0}, use_global_device_ids=true | all-gather | bytes 864 | tf_op jit(solution)/shard_map/all_gather | solution.py:87
  34.5 31.1 %all_gather.52 = bf16[192,768]{0,1:T(8,128)(2,1)S(1)} all-gather(bf16[192,96]{0,1:T(8,128)(2,1)S(1)} %copy.55), channel_id=1, replica_groups=mesh['dp'=8,'tensor'=4] {'dp'}, dimensions={1}, use_global_device_ids=true | all-gather | bytes 331776 | tf_op jit(solution)/shard_map/all_gather | solution.py:88
  65.6 35.3 %all_gather.49 = bf16[3,768,192]{2,0,1:T(4,128)(2,1)} all-gather(bf16[3,96,192]{2,0,1:T(4,128)(2,1)S(1)} %copy.49), channel_id=1, replica_groups=mesh['dp'=8,'tensor'=4] {'dp'}, dimensions={1}, use_global_device_ids=true | all-gather | bytes 995328 | tf_op jit(solution)/shard_map/all_gather | solution.py:86
  114.3 40.8 %while.26 = (s32[]{:T(128)}, bf16[4,512,3,64]{1,3,2,0:T(8,128)(2,1)}, f32[4,3,512,1]{2,1,3,0:T(4,128)}, bf16[3,2,1024,3,64]{2,4,3,1,0:T(8,128)(2,1)S(1)}, s32[4]...) while((s32[]{:T(128)}, ...), condition=%wide.region_3.4_spmd, body=%wide.region_0.3_spmd.sunk | while | flops 422148608 | bytes 25370816 | solution.py:116
  168.6 39.4 %all-reduce.16 = (f32[768]{0:T(1024)}, f32[768]{0:T(1024)}, f32[768]{0:T(1024)S(1)}, f32[768]{0:T(1024)}, f32[768]{0:T(1024)}) all-reduce(f32[768]{0:T(1024)} %dynamic-update-slice.2, f32[768]{0:T(1024)} %dynamic-update-slice.1, f32[768]{0:T(1024)} %dynamic-update-slice, ...), channel_id=1, replica_groups=mesh['dp'=8,'tensor'=4] {'dp','tensor'}, use_global_device_ids=true, to_apply=%add.2 | all-reduce | flops 3840 | bytes 30720
  218.2 21.6 %all-reduce.3 = bf16[768]{0:T(1024)(128)(2,1)} all-reduce(bf16[768]{0:T(1024)(128)(2,1)} %dynamic-update-slice.3), channel_id=1, replica_groups=mesh['dp'=8,'tensor'=4] {'dp'}, use_global_device_ids=true, to_apply=%add.3 | all-reduce | flops 768 | bytes 3072
  243.1 7.0 multiply_convert_fusion.1
  250.1 36.9 %all-gather.13.cloned.1.call-done = bf16[768,768]{0,1:T(8,128)(2,1)} async-done(((bf16[768,96]{0,1:T(8,128)(2,1)}), bf16[768,768]{0,1:T(8,128)(2,1)}) %all-gather.13.cloned.1.call-update) | async-done | bytes 1179664 | tf_op jit(solution)/shard_map/all_gather | solution.py:91
  293.6 36.3 %reduce-scatter.16.cloned.1.call-done = bf16[512,768]{1,0:T(8,128)(2,1)} async-done(((bf16[2048,768]{1,0:T(8,128)(2,1)}), bf16[512,768]{1,0:T(8,128)(2,1)}) %reduce-scatter.16.cloned.1.call-update) | async-done | bytes 786448 | tf_op jit(solution)/shard_map/reduce_scatter | solution.py:135
  337.3 11.4 %collective-permute-done = bf16[512,768]{1,0:T(8,128)(2,1)S(1)} collective-permute-done((bf16[512,768]{1,0:T(8,128)(2,1)S(1)}, bf16[512,768]{1,0:T(8,128)(2,1)S(1)}, u32[]{:S(2)}, u32[]{:S(2)}) %collective-permute-start) | collective-permute-done | bytes 786464 | tf_op jit(solution)/shard_map/ppermute | solution.py:162
  349.6 11.5 %collective-permute-done.1 = bf16[512,768]{1,0:T(8,128)(2,1)} collective-permute-done((bf16[512,768]{1,0:T(8,128)(2,1)S(1)}, bf16[512,768]{1,0:T(8,128)(2,1)}, u32[]{:S(2)}, u32[]{:S(2)}) %collective-permute-start.1) | collective-permute-done | bytes 786464 | tf_op jit(solution)/shard_map/ppermute | solution.py:162
  361.1 11.7 %collective-permute-done.2 = bf16[512,768]{1,0:T(8,128)(2,1)} collective-permute-done((bf16[512,768]{1,0:T(8,128)(2,1)}, bf16[512,768]{1,0:T(8,128)(2,1)}, u32[]{:S(2)}, u32[]{:S(2)}) %collective-permute-start.2) | collective-permute-done | bytes 786464 | tf_op jit(solution)/shard_map/ppermute | solution.py:162
  378.0 8.7 %convert_reduce_fusion = (f32[768]{0:T(1024)}, bf16[2048,768]{1,0:T(8,128)(2,1)S(1)}) fusion(bf16[768,768]{0,1:T(8,128)(2,1)S(1)} %copy-done.48, bf16[4096,768]{1,0:T(8,128)(2,1)S(1)} %constant_dynamic-update-slice_fusion, s32[]{:T(128)S(6)} %select_n.39, f32[2048,768]{1,0:T(8,128)} %get-tuple-element.303, f32[768]{0:T(1024)S(1)} %copy-done.46), kind=kOutput, calls=%fused_computation.66 | convolution fusion | flops 2441084160 | bytes 13769732 | tf_op jit(solution)/shard_map/dot_general | solution.py:58
  392.5 9.6 %all-gather.15.cloned.1.call-start = ((), (), s32[]{:S(2)}) async-start(), calls=%async_computation.15 | async-start | bytes 3932160 | tf_op jit(solution)/shard_map/all_gather | solution.py:183
  402.1 28.5 %reduce-scatter.18.cloned.1.call-done = bf16[512,768]{1,0:T(8,128)(2,1)} async-done(((bf16[2048,768]{1,0:T(8,128)(2,1)}), bf16[512,768]{1,0:T(8,128)(2,1)}) %reduce-scatter.18.cloned.1.call-update) | async-done | bytes 786448 | tf_op jit(solution)/shard_map/reduce_scatter | solution.py:176
  439.0 28.4 %all-gather.15.cloned.1.call-done = bf16[2048,768]{1,0:T(8,128)(2,1)} async-done(((bf16[512,768]{1,0:T(8,128)(2,1)}), bf16[2048,768]{1,0:T(8,128)(2,1)}) %all-gather.15.cloned.1.call-update) | async-done | bytes 3145744 | tf_op jit(solution)/shard_map/all_gather | solution.py:183
  476.4 64.3 %while.27 = (s32[]{:T(128)}, bf16[4,512,3,64]{1,3,2,0:T(8,128)(2,1)}, f32[4,1024,3,64]{1,3,2,0:T(8,128)}, f32[4,1024,3,64]{1,3,2,0:T(8,128)}, bf16[3,2,1024,3,64...) while((s32[]{:T(128)}, ...), condition=%wide.region_17.18_spmd, body=%wide.region_15.17_spmd.sunk | while | flops 1031043584 | bytes 65866036 | solution.py:194
  591.1 7.0 fusion.63
  599.8 40.5 %all-reduce.15 = (f32[768]{0:T(1024)S(1)}, f32[768]{0:T(1024)S(1)}, f32[768]{0:T(1024)S(1)}, f32[768]{0:T(1024)S(1)}, f32[768]{0:T(1024)S(1)}, /*index=5*/f32[768]{0:T(1024)S(1)}, f32[768]{0:T(1024)S(1)}) all-reduce(f32[768]{0:T(1024)S(1)} %dynamic-update-slice.6, ...), channel_id=1, replica_groups=mesh['dp'=8,'tensor'=4] {'dp','tensor'}, use_global_device_ids=true, to_apply=%add.6 | all-reduce | flops 5376 | bytes 43008
  645.4 21.3 %all-reduce.17 = (f32[2,192]{1,0:T(2,128)S(1)}, f32[768]{0:T(1024)S(1)}) all-reduce(f32[2,192]{1,0:T(2,128)S(1)} %pad_maximum_fusion, f32[768]{0:T(1024)S(1)} %copy-done.45), channel_id=7, replica_groups=mesh['dp'=8,'tensor'=4] {'dp'}, use_global_device_ids=true, to_apply=%region_23.24.clone | all-reduce | flops 1152 | bytes 9216
  669.6 7.7 reduce-scatter.26.cloned.1.call-done
  679.2 37.5 %reduce-scatter.20.cloned.1.call-done = bf16[512,768]{1,0:T(8,128)(2,1)} async-done(((bf16[2048,768]{1,0:T(8,128)(2,1)}), bf16[512,768]{1,0:T(8,128)(2,1)}) %reduce-scatter.20.cloned.1.call-update) | async-done | bytes 786448 | tf_op jit(solution)/shard_map/reduce_scatter | solution.py:210
  718.9 70.6 %reduce-scatter.22.cloned.1.call-done = f32[96,768]{1,0:T(8,128)} async-done(((f32[768,768]{1,0:T(8,128)}), f32[96,768]{1,0:T(8,128)}) %reduce-scatter.22.cloned.1.call-update) | async-done | bytes 294928 | tf_op jit(solution)/shard_map/reduce_scatter | solution.py:222
  789.6 72.3 %reduce-scatter.24.cloned.1.call-done = f32[768,96]{0,1:T(8,128)} async-done(((f32[768,768]{0,1:T(8,128)}), f32[768,96]{0,1:T(8,128)}) %reduce-scatter.24.cloned.1.call-update) | async-done | bytes 294928 | tf_op jit(solution)/shard_map/reduce_scatter | solution.py:224
  (342 shorter events, 238.3 us)
Async XLA Ops:
  8.0 92.9 %all-gather.7.cloned.1.call-start = ((), (), s32[]{:S(2)}) async-start(), calls=%async_computation.8 | async-start | bytes 3932160 | tf_op jit(solution)/shard_map/all_gather | solution.py:103
  8.7 199.2 %reduce-scatter.14.cloned.1.call-start = ((), (), s32[]{:S(2)}) async-start(), calls=%async_computation.9 | async-start | bytes 3932160 | tf_op jit(solution)/shard_map/reduce_scatter | solution.py:120
  158.2 49.8 %copy-start.2 = (bf16[512,768]{1,0:T(8,128)(2,1)S(1)}, bf16[512,768]{1,0:T(8,128)(2,1)}, u32[]{:S(2)}) copy-start(bf16[512,768]{1,0:T(8,128)(2,1)} %param.19) | copy-start | bytes 2359300
  161.0 80.1 %all-gather.11.cloned.1.call-start = ((), (), s32[]{:S(2)}) async-start(), calls=%async_computation.11 | async-start | bytes 1327104 | tf_op jit(solution)/shard_map/all_gather | solution.py:89
  161.5 81.6 %all-gather.9.cloned.1.call-start = ((), (), s32[]{:S(2)}) async-start(), calls=%async_computation.10 | async-start | bytes 3932160 | tf_op jit(solution)/shard_map/all_gather | solution.py:130
  213.6 73.3 %all-gather.13.cloned.1.call-start = ((), (), s32[]{:S(2)}) async-start(), calls=%async_computation.12 | async-start | bytes 1327104 | tf_op jit(solution)/shard_map/all_gather | solution.py:91
  214.2 115.7 %reduce-scatter.16.cloned.1.call-start = ((), (), s32[]{:S(2)}) async-start(), calls=%async_computation.13 | async-start | bytes 3932160 | tf_op jit(solution)/shard_map/reduce_scatter | solution.py:135
  293.5 137.1 %reduce-scatter.18.cloned.1.call-start = ((), (), s32[]{:S(2)}) async-start(), calls=%async_computation.14 | async-start | bytes 3932160 | tf_op jit(solution)/shard_map/reduce_scatter | solution.py:176
  337.3 11.4 %collective-permute-start = (bf16[512,768]{1,0:T(8,128)(2,1)S(1)}, bf16[512,768]{1,0:T(8,128)(2,1)S(1)}, u32[]{:S(2)}, u32[]{:S(2)}) collective-permute-start(bf16[512,768]{1,0:T(8,128)(2,1)S(1)} %get-tuple-element.279), channel_id=1, source_target_pairs={{0,1},{1,2},{2,3},{3,0},{4,5},{5,6},{6,7},{7,4},{8,9},{9,10},{10,1... | collective-permute-start | bytes 2359304 | tf_op jit(solution)/shard_map/ppermute | solution.py:162
  349.6 11.5 %collective-permute-start.1 = (bf16[512,768]{1,0:T(8,128)(2,1)S(1)}, bf16[512,768]{1,0:T(8,128)(2,1)}, u32[]{:S(2)}, u32[]{:S(2)}) collective-permute-start(bf16[512,768]{1,0:T(8,128)(2,1)S(1)} %collective-permute-done), channel_id=1, source_target_pairs={{0,1},{1,2},{2,3},{3,0},{4,5},{5,6},{6,7},{7,4},{8,9},{9,10},{10,1... | collective-permute-start | bytes 2359304 | tf_op jit(solution)/shard_map/ppermute | solution.py:162
  361.1 11.7 %collective-permute-start.2 = (bf16[512,768]{1,0:T(8,128)(2,1)}, bf16[512,768]{1,0:T(8,128)(2,1)}, u32[]{:S(2)}, u32[]{:S(2)}) collective-permute-start(bf16[512,768]{1,0:T(8,128)(2,1)} %collective-permute-done.1), channel_id=1, source_target_pairs={{0,1},{1,2},{2,3},{3,0},{4,5},{5,6},{6,7},{7,4},{8,9},{9,10},{10,1... | collective-permute-start | bytes 2359304 | tf_op jit(solution)/shard_map/ppermute | solution.py:162
  392.5 74.8 %all-gather.15.cloned.1.call-start = ((), (), s32[]{:S(2)}) async-start(), calls=%async_computation.15 | async-start | bytes 3932160 | tf_op jit(solution)/shard_map/all_gather | solution.py:183
  438.9 229.1 %reduce-scatter.28.cloned.1.call-start = ((), (), s32[]{:S(2)}) async-start(), calls=%async_computation.20 | async-start | bytes 884736
  438.9 37.5 %copy-start.8 = (bf16[4,512,3,64]{1,3,2,0:T(8,128)(2,1)S(1)}, bf16[4,512,3,64]{1,3,2,0:T(8,128)(2,1)}, u32[]{:S(2)}) copy-start(bf16[4,512,3,64]{1,3,2,0:T(8,128)(2,1)} %copy-done.7) | copy-start | bytes 2359300
  545.3 132.0 %reduce-scatter.26.cloned.1.call-start = ((), (), s32[]{:S(2)}) async-start(), calls=%async_computation.19 | async-start | bytes 2211840
  578.0 138.7 %reduce-scatter.20.cloned.1.call-start = ((), (), s32[]{:S(2)}) async-start(), calls=%async_computation.16 | async-start | bytes 3932160 | tf_op jit(solution)/shard_map/reduce_scatter | solution.py:210
  583.7 205.9 %reduce-scatter.22.cloned.1.call-start = ((), (), s32[]{:S(2)}) async-start(), calls=%async_computation.17 | async-start | bytes 2654208 | tf_op jit(solution)/shard_map/reduce_scatter | solution.py:222
  591.0 52.8 %copy-start.31 = (f32[512]{0:T(512)S(1)}, f32[512]{0:T(512)}, u32[]{:S(2)}) copy-start(f32[512]{0:T(512)} %copy-done.30) | copy-start | bytes 6148
  591.0 52.8 %copy-start.33 = (f32[768]{0:T(1024)S(1)}, f32[768]{0:T(1024)}, u32[]{:S(2)}) copy-start(f32[768]{0:T(1024)} %get-tuple-element.275) | copy-start | bytes 9220
  591.0 52.8 %copy-start.36 = (f32[512]{0:T(512)S(1)}, f32[512]{0:T(512)}, u32[]{:S(2)}) copy-start(f32[512]{0:T(512)} %copy-done.35) | copy-start | bytes 6148
  591.0 270.8 %reduce-scatter.24.cloned.1.call-start = ((), (), s32[]{:S(2)}) async-start(), calls=%async_computation.18 | async-start | bytes 2654208 | tf_op jit(solution)/shard_map/reduce_scatter | solution.py:224
  598.0 45.7 %copy-start.1 = (f32[512,768]{1,0:T(8,128)S(1)}, f32[512,768]{1,0:T(8,128)}, u32[]{:S(2)}) copy-start(f32[512,768]{1,0:T(8,128)} %copy-done) | copy-start | bytes 4718596
  598.0 47.3 %copy-start.45 = (f32[768]{0:T(1024)S(1)}, f32[768]{0:T(1024)}, u32[]{:S(2)}) copy-start(f32[768]{0:T(1024)} %get-tuple-element.304) | copy-start | bytes 9220
  645.0 71.7 %copy-start.10 = (f32[512,768]{1,0:T(8,128)S(1)}, f32[512,768]{1,0:T(8,128)}, u32[]{:S(2)}) copy-start(f32[512,768]{1,0:T(8,128)} %copy-done.9) | copy-start | bytes 4718596
  (53 other events, 242.6 us)
Sparse Core Ops, SparseCore 0:
  10.4 31.2 all-gather.6
  161.1 36.9 reduce-scatter.13
  392.6 37.9 reduce-scatter.17
Sparse Core Ops, SparseCore 1:
  163.6 40.1 all-gather.10
  213.7 29.3 all-gather.8
  245.4 41.5 all-gather.12
  293.6 36.3 reduce-scatter.15
  438.9 28.3 all-gather.14
  545.3 62.5 reduce-scatter.27
  611.2 66.0 reduce-scatter.25
  679.9 36.8 reduce-scatter.19
  720.6 68.9 reduce-scatter.21
  793.6 68.1 reduce-scatter.23
